TPU v7x, 256 devices: a whole 4x4x8 slice. The times are simulated.
256 devices in a mesh: fsdp: 16 (over x_lo, z), expert: 16 (over y, x_hi, core).
Axes of the slice: x: 4 (x_hi: 2, x_lo: 2; x = x_hi * 2 + x_lo), y: 4, z: 8, core: 2. Of those that a mesh axis runs over, the one named last changes fastest.
Arguments:
- tokens: bfloat16 [2048, 3072], P('expert'), may hold values from -6 to 6
- cotangent: bfloat16 [2048, 3072], P('expert'), may hold values from -6 to 6
- expert_ids: int32 [2048, 4], P('expert'), may hold values from 0 to 15, all different within a row; in each aligned block of 128 rows (0 to 127, 128 to 255, ...) at most 40 rows name the same one
- gate_values: bfloat16 [2048, 4], P('expert'), may hold values from 0.049804688 to 0.5
- w_in: bfloat16 [3072, 16, 6144], P(None, 'expert', 'fsdp'), may hold values from -0.109375 to 0.109375
- w_out: bfloat16 [6144, 16, 3072], P('fsdp', 'expert'), may hold values from -0.078125 to 0.078125
Outputs:
- grad_tokens: bfloat16 [2048, 3072], P('expert')
- grad_gates: bfloat16 [2048, 4], P('expert')
- grad_w_in: bfloat16 [3072, 16, 6144], P(None, 'expert', 'fsdp')
- grad_w_out: bfloat16 [6144, 16, 3072], P('fsdp', 'expert')
Inputs may be any that keep to these rules, and one draw needn't show every extreme that they name: `expert_ids`: in each aligned block of 128 rows (the rows of one index of the expert axis) the 4 entries of a row differ, no expert is named by more than 40 rows, a bound that some block reaches.
All inputs are finite; a program needn't handle non-finite values.
Results may differ from a plain program's by a relative error of at most 0.0049.
Values may be sent and summed in bfloat16 or wider, within the bound.
A program may use at most 128 MiB of HBM per device.

v0:
```python
import jax
import jax.numpy as jnp
from jax import lax
from jax.sharding import PartitionSpec as P

EXPERTS = 16
CAP = 40
F32 = jnp.float32
BF16 = jnp.bfloat16


def local(tokens, cotangent, expert_ids, gate_values, w_in, w_out):
    rows, width = tokens.shape
    n_f = lax.axis_size("fsdp")
    part = 2 * width // n_f
    me_f = lax.axis_index("fsdp")
    half = me_f // (n_f // 2)
    col = me_f % (n_f // 2) * part
    ids_t = expert_ids.T
    experts = jnp.arange(EXPERTS, dtype=jnp.int32)[:, None]
    hit = ids_t[None] == experts[:, :, None]
    named = jnp.any(hit, axis=1)
    gates_of = jnp.sum(jnp.where(hit, gate_values.T[None].astype(F32), 0.0), axis=1)
    before = jnp.arange(rows)[:, None] < jnp.arange(rows)[None, :]
    place = jnp.dot(named.astype(BF16), before.astype(BF16), preferred_element_type=F32).astype(
        jnp.int32
    )
    slots = jnp.arange(CAP, dtype=jnp.int32)[None, :, None]
    pick = ((place[:, None, :] == slots) & named[:, None, :]).reshape(EXPERTS * CAP, rows)
    pick_b = pick.astype(BF16)
    gate_send = jnp.sum(
        jnp.where(pick.reshape(EXPERTS, CAP, rows), gates_of[:, None, :], 0.0), axis=2
    )
    chosen = jnp.where(
        half == 0,
        lax.dynamic_slice_in_dim(tokens, col, part, 1),
        lax.dynamic_slice_in_dim(cotangent, col, part, 1),
    )
    send = jnp.dot(pick_b, chosen, preferred_element_type=F32).astype(BF16)
    send = send.reshape(EXPERTS, CAP, part)
    got = lax.all_to_all(send, "expert", split_axis=0, concat_axis=0, tiled=True)
    gate_got = lax.all_to_all(gate_send, "expert", split_axis=0, concat_axis=0, tiled=True)
    every = lax.all_gather(got.reshape(EXPERTS * CAP, part), "fsdp", axis=0)
    xs, gs = (every[: n_f // 2], every[n_f // 2 :])
    win = w_in.reshape(n_f // 2, part, -1)
    wout = w_out.reshape(-1, n_f // 2, part)
    pre = jnp.einsum("zsd,zdf->sf", xs, win, preferred_element_type=F32)
    up = jnp.einsum("zsd,fzd->sf", gs, wout, preferred_element_type=F32)
    gate = gate_got.reshape(EXPERTS * CAP, 1)
    squash = jax.nn.sigmoid(pre)
    active = pre * squash
    gate_part = jnp.sum(active * up, axis=-1)
    act_gated = (gate * active).astype(BF16)
    grad_pre = (gate * squash * (1.0 + pre * (1.0 - squash)) * up).astype(BF16)
    w16 = w_in.reshape(n_f, width // n_f, -1)
    part_x = jnp.einsum("sf,zdf->zsd", grad_pre, w16, preferred_element_type=F32)
    mine = lax.psum_scatter(part_x, "fsdp", scatter_dimension=0, tiled=False)
    gate_sum = lax.psum(gate_part.reshape(EXPERTS, CAP), "fsdp")
    back_x = lax.all_to_all(mine.reshape(EXPERTS, CAP, -1), "expert", 0, 0, tiled=True)
    back_gate = lax.all_to_all(gate_sum, "expert", split_axis=0, concat_axis=0, tiled=True)
    grad_in = jnp.einsum("zsd,sf->zdf", xs, grad_pre, preferred_element_type=F32).astype(BF16)
    grad_out = jnp.einsum("sf,zsd->fzd", act_gated, gs, preferred_element_type=F32).astype(BF16)
    tok = jnp.dot(
        pick.astype(F32).T,
        back_x.reshape(EXPERTS * CAP, -1),
        precision=lax.Precision.HIGHEST,
        preferred_element_type=F32,
    ).astype(BF16)
    grad_tokens = lax.all_gather(tok, "fsdp", axis=1, tiled=True)
    by_expert = jnp.sum(
        jnp.where(pick.reshape(EXPERTS, CAP, rows), back_gate[:, :, None], 0.0), axis=1
    )
    grad_gates = jnp.sum(jnp.where(hit, by_expert[:, None, :], 0.0), axis=0).T.astype(BF16)
    return (grad_tokens, grad_gates, grad_in.reshape(w_in.shape), grad_out.reshape(w_out.shape))


def solution(mesh):
    return jax.shard_map(
        local,
        mesh=mesh,
        in_specs=(
            P("expert", None),
            P("expert", None),
            P("expert", None),
            P("expert", None),
            P(None, "expert", "fsdp"),
            P("fsdp", "expert", None),
        ),
        out_specs=(
            P("expert", None),
            P("expert", None),
            P(None, "expert", "fsdp"),
            P("fsdp", "expert", None),
        ),
        check_vma=False,
    )
```

profile of v0, /device:TPU:2, one launch (start us, length us, event | category | flops | bytes accessed | tf_op | source)
XLA Modules:
  0.0 350.6 jit_solution(9001200368042260039)
XLA Ops:
  7.3 0.8 fusion.27
  8.5 1.2 convolution_convert_fusion.1
  9.7 18.0 %all_to_all.28 = bf16[16,40,384]{2,1,0:T(8,128)(2,1)} all-to-all(bf16[16,40,384]{2,1,0:T(8,128)(2,1)S(1)} %bitcast.59), channel_id=1, replica_groups=mesh['fsdp'=16,'expert'=16] {'expert'}, dimensions={0} | all-to-all | bytes 983040 | tf_op jit(solution)/shard_map/all_to_all | solution.py:41
  27.8 3.6 %copy.59 = bf16[48,8,8,384]{3,2,1,0:T(8,128)(2,1)} copy(bf16[48,8,8,384]{3,1,2,0:T(8,128)(2,1)} %bitcast.55) | data formatting | bytes 4718592
  31.4 90.4 %all-gather.2.cloned.1.call-done = bf16[16,640,384]{2,1,0:T(8,128)(2,1)} async-done(((bf16[1,640,384]{2,1,0:T(8,128)(2,1)}), bf16[16,640,384]{2,1,0:T(8,128)(2,1)}) %all-gather.2.cloned.1.call-update) | async-done | bytes 7864336 | tf_op jit(solution)/shard_map/all_gather | solution.py:43
  121.8 4.3 %convolution_bitcast_fusion.1 = f32[640,384]{0,1:T(8,128)S(1)} fusion(bf16[16,640,384]{2,1,0:T(8,128)(2,1)} %all-gather.2.cloned.1.call-done, bf16[8,384,384]{2,1,0:T(8,128)(2,1)S(1)} %bitcast.53), kind=kOutput, calls=%fused_computation.8 | convolution fusion | flops 1509949440 | bytes 11206656 | tf_op jit(solution)/shard_map/zsd,zdf->sf/dot_general | solution.py:47
  126.1 0.8 copy-done.5
  127.0 3.0 multiply_reduce_fusion
  130.0 33.5 %psum.7 = f32[16,1,40]{2,1,0:T(1,128)} all-reduce(f32[16,1,40]{2,1,0:T(1,128)S(1)} %all_to_all.22), channel_id=1, replica_groups=mesh['fsdp'=16,'expert'=16] {'fsdp'}, use_global_device_ids=true, to_apply=%region_5.6 | all-reduce | flops 640 | bytes 5120 | tf_op jit(solution)/shard_map/psum | solution.py:58
  163.5 6.2 %all-to-all-start.3 = ((f32[16,1,40]{2,1,0:T(1,128)}), f32[16,1,40]{2,1,0:T(1,128)S(1)}, u32[]{:S(2)}, u32[]{:S(2)}) async-start(f32[16,1,40]{2,1,0:T(1,128)} %psum.7), calls=%async_computation.4 | async-start | bytes 16384 | tf_op jit(solution)/shard_map/all_to_all | solution.py:60
  169.8 7.4 %all-to-all-done.3 = f32[16,1,40]{2,1,0:T(1,128)S(1)} async-done(((f32[16,1,40]{2,1,0:T(1,128)}), f32[16,1,40]{2,1,0:T(1,128)S(1)}, u32[]{:S(2)}, u32[]{:S(2)}) %all-to-all-start.3) | async-done | bytes 2592 | tf_op jit(solution)/shard_map/all_to_all | solution.py:60
  177.5 10.1 %all_to_all.29 = f32[16,1,40]{2,1,0:T(1,128)S(1)} all-to-all(f32[16,1,40]{2,1,0:T(1,128)S(1)} %bitcast.61), channel_id=1, replica_groups=mesh['fsdp'=16,'expert'=16] {'expert'}, dimensions={0} | all-to-all | bytes 5120 | tf_op jit(solution)/shard_map/all_to_all | solution.py:42
  188.9 1.9 multiply_convert_fusion.1
  190.8 4.6 %convolution_bitcast_fusion = f32[16,640,192]{1,2,0:T(8,128)} fusion(bf16[16,192,384]{2,1,0:T(8,128)(2,1)S(1)} %bitcast.52, bf16[640,384]{0,1:T(8,128)(2,1)S(1)} %multiply_convert_fusion.1), kind=kOutput, calls=%fused_computation.2 | convolution fusion | flops 1509949440 | bytes 10715136 | tf_op jit(solution)/shard_map/sf,zdf->zsd/dot_general | solution.py:56
  196.0 6.3 %fusion.4 = bf16[384,8,384]{0,2,1:T(8,128)(2,1)} fusion(bf16[16,640,384]{2,1,0:T(8,128)(2,1)} %all-gather.2.cloned.1.call-done, f32[640]{0:T(1024)S(1)} %mul.34, f32[640,384]{0,1:T(8,128)} %copy-done.2), kind=kOutput, calls=%fused_computation.5 | convolution fusion | flops 1512603648 | bytes 7277056 | tf_op jit(solution)/shard_map/sf,zsd->fzd/dot_general | solution.py:62
  202.3 4.3 %copy.49 = bf16[384,1,3072]{2,0,1:T(8,128)(2,1)} copy(bf16[384,1,3072]{0,2,1:T(8,128)(2,1)} %bitcast.57) | data formatting | bytes 4718592
  206.5 77.1 %reduce-scatter.2.cloned.1.call-done = f32[1,640,192]{1,2,0:T(8,128)} async-done(((f32[16,640,192]{1,2,0:T(8,128)}), f32[1,640,192]{1,2,0:T(8,128)}) %reduce-scatter.2.cloned.1.call-update) | async-done | bytes 491536 | tf_op jit(solution)/shard_map/reduce_scatter | solution.py:57
  283.6 2.1 copy.43
  285.7 6.2 %all-to-all-start.2 = ((f32[16,40,192]{2,1,0:T(8,128)}), f32[16,40,192]{2,1,0:T(8,128)S(1)}, u32[]{:S(2)}, u32[]{:S(2)}) async-start(f32[16,40,192]{2,1,0:T(8,128)} %bitcast.54), calls=%async_computation.3 | async-start | bytes 1310720 | tf_op jit(solution)/shard_map/all_to_all | solution.py:59
  291.9 6.0 %convolution_convert_fusion = bf16[8,384,384]{2,1,0:T(8,128)(2,1)} fusion(bf16[16,640,384]{2,1,0:T(8,128)(2,1)} %all-gather.2.cloned.1.call-done, bf16[640,384]{0,1:T(8,128)(2,1)S(1)} %multiply_convert_fusion.1), kind=kOutput, calls=%fused_computation.6 | convolution fusion | flops 1511129088 | bytes 10715136 | tf_op jit(solution)/shard_map/zsd,sf->zdf/dot_general | solution.py:61
  297.9 7.8 %all-to-all-done.2 = f32[16,40,192]{2,1,0:T(8,128)S(1)} async-done(((f32[16,40,192]{2,1,0:T(8,128)}), f32[16,40,192]{2,1,0:T(8,128)S(1)}, u32[]{:S(2)}, u32[]{:S(2)}) %all-to-all-start.2) | async-done | bytes 491552 | tf_op jit(solution)/shard_map/all_to_all | solution.py:59
  305.7 0.7 fusion.10
  306.4 36.2 %all_gather.7 = bf16[128,3072]{0,1:T(8,128)(2,1)S(1)} all-gather(bf16[128,192]{0,1:T(8,128)(2,1)S(1)} %fusion.10), channel_id=1, replica_groups=mesh['fsdp'=16,'expert'=16] {'fsdp'}, dimensions={1}, use_global_device_ids=true | all-gather | bytes 835584 | tf_op jit(solution)/shard_map/all_gather | solution.py:69
  342.6 1.2 copy.48
  (27 shorter events, 2.7 us)
Async XLA Ops:
  7.2 114.7 %copy-start = (bf16[3072,1,384]{2,0,1:T(8,128)(2,1)S(1)}, bf16[3072,1,384]{2,0,1:T(8,128)(2,1)}, u32[]{:S(2)}) copy-start(bf16[3072,1,384]{2,0,1:T(8,128)(2,1)} %param.10) | copy-start | bytes 7077892
  7.2 24.2 %copy-start.4 = (bf16[128,4]{0,1:T(4,128)(2,1)S(1)}, bf16[128,4]{0,1:T(4,128)(2,1)}, u32[]{:S(2)}) copy-start(bf16[128,4]{0,1:T(4,128)(2,1)} %param.9) | copy-start | bytes 3076
  7.2 114.6 %all-gather.2.cloned.1.call-start = ((), (), s32[]{:S(2)}) async-start(), calls=%async_computation.5 | async-start | bytes 8355840 | tf_op jit(solution)/shard_map/all_gather | solution.py:43
  121.8 4.3 %copy-start.1 = (bf16[48,8,8,384]{3,2,1,0:T(8,128)(2,1)S(1)}, bf16[48,8,8,384]{3,2,1,0:T(8,128)(2,1)}, u32[]{:S(2)}) copy-start(bf16[48,8,8,384]{3,2,1,0:T(8,128)(2,1)} %copy.59) | copy-start | bytes 7077892
  121.8 5.1 %copy-start.5 = (bf16[16,640,384]{2,1,0:T(8,128)(2,1)S(1)}, bf16[16,640,384]{2,1,0:T(8,128)(2,1)}, u32[]{:S(2)}) copy-start(bf16[16,640,384]{2,1,0:T(8,128)(2,1)} %all-gather.2.cloned.1.call-done) | copy-start | bytes 23592964
  126.1 3.8 %copy-start.2 = (f32[640,384]{0,1:T(8,128)}, f32[640,384]{0,1:T(8,128)S(1)}, u32[]{:S(2)}) copy-start(f32[640,384]{0,1:T(8,128)S(1)} %convolution_bitcast_fusion.1) | copy-start | bytes 2949124
  127.0 42.8 %copy-start.3 = (s32[128,4]{0,1:T(4,128)S(1)}, s32[128,4]{0,1:T(4,128)}, u32[]{:S(2)}) copy-start(s32[128,4]{0,1:T(4,128)} %param.8) | copy-start | bytes 6148
  163.5 13.7 %all-to-all-start.3 = ((f32[16,1,40]{2,1,0:T(1,128)}), f32[16,1,40]{2,1,0:T(1,128)S(1)}, u32[]{:S(2)}, u32[]{:S(2)}) async-start(f32[16,1,40]{2,1,0:T(1,128)} %psum.7), calls=%async_computation.4 | async-start | bytes 16384 | tf_op jit(solution)/shard_map/all_to_all | solution.py:60
  169.7 113.9 %reduce-scatter.2.cloned.1.call-start = ((), (), s32[]{:S(2)}) async-start(), calls=%async_computation.6 | async-start | bytes 8355840 | tf_op jit(solution)/shard_map/reduce_scatter | solution.py:57
  285.7 20.0 %all-to-all-start.2 = ((f32[16,40,192]{2,1,0:T(8,128)}), f32[16,40,192]{2,1,0:T(8,128)S(1)}, u32[]{:S(2)}, u32[]{:S(2)}) async-start(f32[16,40,192]{2,1,0:T(8,128)} %bitcast.54), calls=%async_computation.3 | async-start | bytes 1310720 | tf_op jit(solution)/shard_map/all_to_all | solution.py:59
Sparse Core Ops, SparseCore 0:
  27.9 93.8 all-gather.1
  195.5 88.0 reduce-scatter.1
where the time goes:
time: 351 us
  waiting for transfers between devices  183 us (52%)
  blocking collectives  97.8 us (28%)
  matrix products  26.2 us (7%)
  between operations  14.2 us (4%)
  local copies, waits for them, and re-layouts  12.7 us (4%)
  starting transfers between devices  12.5 us (4%)
  other arithmetic  4.41 us (1%)
    all_gather x1, waiting for transfers between devices, local(): every = lax.all_gather(got.reshape(EXPERTS * CAP, part), 'fsdp', axis=0)  90.4 us
    reduce_scatter x1, waiting for transfers between devices, local(): mine = lax.psum_scatter(part_x, 'fsdp', scatter_dimension=0, tiled=False)  77.1 us
    all_gather x1, blocking collectives, local(): grad_tokens = lax.all_gather(tok, 'fsdp', axis=1, tiled=True)  36.2 us
    psum x1, blocking collectives, local(): gate_sum = lax.psum(gate_part.reshape(EXPERTS, CAP), 'fsdp')  33.5 us
    all_to_all x1, blocking collectives, local(): lax.all_to_all(send, 'expert', split_axis=0, concat_axis=0, tiled=True)  18 us
    all_to_all x1, blocking collectives, local(): lax.all_to_all(gate_send, 'expert', split_axis=0, concat_axis=0, tiled=True)  10.1 us
    unnamed x15, local copies, waits for them, and re-layouts  9.86 us
    all_to_all x1, waiting for transfers between devices, local(): lax.all_to_all(mine.reshape(EXPERTS, CAP, -1), 'expert', 0, 0, tiled=True)  7.79 us
  transfers between devices with their start and end apart: 4, of which 4 were waited for; matrix products, arithmetic and copies ran while one was open for 6% of the time, Pallas kernels for 0%

commit v1 on v0

--- a/solution.py
+++ b/solution.py
@@ -66,7 +66,12 @@
         precision=lax.Precision.HIGHEST,
         preferred_element_type=F32,
     ).astype(BF16)
-    grad_tokens = lax.all_gather(tok, "fsdp", axis=1, tiled=True)
+    sides = []
+    for _ in range(lax.axis_size("fsdp")):
+        sides.append(tok)
+    grad_tokens = jnp.concatenate(
+        lax.all_to_all(jnp.stack(sides, axis=0), concat_axis=0, split_axis=0, axis_name="fsdp"), 1
+    )
     by_expert = jnp.sum(
         jnp.where(pick.reshape(EXPERTS, CAP, rows), back_gate[:, :, None], 0.0), axis=1
     )

time: 351 us -> 342 us (0.974)
  blocking collectives: 97.8 us -> 81.4 us
  waiting for transfers between devices: 183 us -> 189 us
    all_gather x1 -> x0, blocking collectives: 36.2 us -> none  [local(): grad_tokens = lax.all_gather(tok, 'fsdp', axis=1, tiled=True)]
    all_to_all x0 -> x1, blocking collectives: none -> 19.8 us  [local(): lax.all_to_all(mine.reshape(EXPERTS, CAP, -1), 'expert', 0, 0, tiled=True)]
    reduce_scatter x1, waiting for transfers between devices: 77.1 us -> 88.2 us  [local(): mine = lax.psum_scatter(part_x, 'fsdp', scatter_dimension=0, tiled=False)]
    all_to_all x1, waiting for transfers between devices: 7.79 us -> 2.52 us  [local(): lax.all_to_all(jnp.stack(sides, axis=0), concat_axis=0, split_axis=0, axi...]
    unnamed x15 -> x17, local copies, waits for them, and re-layouts: 9.86 us -> 10.6 us
where the time goes in v1:
time: 342 us; the launch traced here: 340 us
  waiting for transfers between devices  189 us (55%)
  blocking collectives  81.4 us (24%)
  matrix products  26.3 us (8%)
  between operations  14.2 us (4%)
  local copies, waits for them, and re-layouts  13.7 us (4%)
  starting transfers between devices  12 us (4%)
  other arithmetic  4.11 us (1%)
    all_gather x1, waiting for transfers between devices, local(): every = lax.all_gather(got.reshape(EXPERTS * CAP, part), 'fsdp', axis=0)  90.4 us
    reduce_scatter x1, waiting for transfers between devices, local(): mine = lax.psum_scatter(part_x, 'fsdp', scatter_dimension=0, tiled=False)  88.2 us
    psum x1, blocking collectives, local(): gate_sum = lax.psum(gate_part.reshape(EXPERTS, CAP), 'fsdp')  33.5 us
    all_to_all x1, blocking collectives, local(): lax.all_to_all(mine.reshape(EXPERTS, CAP, -1), 'expert', 0, 0, tiled=True)  19.8 us
    all_to_all x1, blocking collectives, local(): lax.all_to_all(send, 'expert', split_axis=0, concat_axis=0, tiled=True)  18 us
    unnamed x17, local copies, waits for them, and re-layouts  10.6 us
    all_to_all x1, blocking collectives, local(): lax.all_to_all(gate_send, 'expert', split_axis=0, concat_axis=0, tiled=True)  10.1 us
    all_to_all x1, waiting for transfers between devices, local(): lax.all_to_all(gate_sum, 'expert', split_axis=0, concat_axis=0, tiled=True)  7.43 us
  transfers between devices with their start and end apart: 4, of which 4 were waited for; matrix products, arithmetic and copies ran while one was open for 6% of the time, Pallas kernels for 0%

profile of v1, /device:TPU:2, one launch (start us, length us, event | category | flops | bytes accessed | tf_op | source)
XLA Modules:
  0.0 340.4 jit_solution(2988691049170488927)
XLA Ops:
  7.3 0.8 fusion.27
  8.5 1.2 convolution_convert_fusion.1
  9.7 18.0 %all_to_all.33 = bf16[16,40,384]{2,1,0:T(8,128)(2,1)} all-to-all(bf16[16,40,384]{2,1,0:T(8,128)(2,1)S(1)} %bitcast.63), channel_id=1, replica_groups=mesh['fsdp'=16,'expert'=16] {'expert'}, dimensions={0} | all-to-all | bytes 983040 | tf_op jit(solution)/shard_map/all_to_all | solution.py:41
  27.8 3.6 %copy.59 = bf16[48,8,8,384]{3,2,1,0:T(8,128)(2,1)} copy(bf16[48,8,8,384]{3,1,2,0:T(8,128)(2,1)} %bitcast.59) | data formatting | bytes 4718592
  31.4 90.4 %all-gather.2.cloned.1.call-done = bf16[16,640,384]{2,1,0:T(8,128)(2,1)} async-done(((bf16[1,640,384]{2,1,0:T(8,128)(2,1)}), bf16[16,640,384]{2,1,0:T(8,128)(2,1)}) %all-gather.2.cloned.1.call-update) | async-done | bytes 7864336 | tf_op jit(solution)/shard_map/all_gather | solution.py:43
  121.8 4.3 %convolution_bitcast_fusion.1 = f32[640,384]{0,1:T(8,128)S(1)} fusion(bf16[16,640,384]{2,1,0:T(8,128)(2,1)} %all-gather.2.cloned.1.call-done, bf16[8,384,384]{2,1,0:T(8,128)(2,1)S(1)} %bitcast.56), kind=kOutput, calls=%fused_computation.8 | convolution fusion | flops 1509949440 | bytes 11206656 | tf_op jit(solution)/shard_map/zsd,zdf->sf/dot_general | solution.py:47
  126.1 0.8 copy-done.6
  127.0 3.0 multiply_reduce_fusion
  130.0 33.5 %psum.7 = f32[16,1,40]{2,1,0:T(1,128)} all-reduce(f32[16,1,40]{2,1,0:T(1,128)S(1)} %all_to_all.26), channel_id=1, replica_groups=mesh['fsdp'=16,'expert'=16] {'fsdp'}, use_global_device_ids=true, to_apply=%region_5.6 | all-reduce | flops 640 | bytes 5120 | tf_op jit(solution)/shard_map/psum | solution.py:58
  163.5 6.2 %all-to-all-start.4 = ((f32[16,1,40]{2,1,0:T(1,128)}), f32[16,1,40]{2,1,0:T(1,128)S(1)}, u32[]{:S(2)}, u32[]{:S(2)}) async-start(f32[16,1,40]{2,1,0:T(1,128)} %psum.7), calls=%async_computation.5 | async-start | bytes 16384 | tf_op jit(solution)/shard_map/all_to_all | solution.py:60
  169.8 7.4 %all-to-all-done.4 = f32[16,1,40]{2,1,0:T(1,128)S(1)} async-done(((f32[16,1,40]{2,1,0:T(1,128)}), f32[16,1,40]{2,1,0:T(1,128)S(1)}, u32[]{:S(2)}, u32[]{:S(2)}) %all-to-all-start.4) | async-done | bytes 2592 | tf_op jit(solution)/shard_map/all_to_all | solution.py:60
  177.5 10.1 %all_to_all.34 = f32[16,1,40]{2,1,0:T(1,128)S(1)} all-to-all(f32[16,1,40]{2,1,0:T(1,128)S(1)} %bitcast.65), channel_id=1, replica_groups=mesh['fsdp'=16,'expert'=16] {'expert'}, dimensions={0} | all-to-all | bytes 5120 | tf_op jit(solution)/shard_map/all_to_all | solution.py:42
  188.9 1.6 multiply_convert_fusion.1
  191.3 4.5 %convolution_bitcast_fusion = f32[16,640,192]{1,2,0:T(8,128)} fusion(bf16[16,192,384]{2,1,0:T(8,128)(2,1)S(1)} %bitcast.55, bf16[640,384]{0,1:T(8,128)(2,1)S(1)} %multiply_convert_fusion.1), kind=kOutput, calls=%fused_computation.2 | convolution fusion | flops 1509949440 | bytes 10715136 | tf_op jit(solution)/shard_map/sf,zdf->zsd/dot_general | solution.py:56
  195.8 88.2 %reduce-scatter.2.cloned.1.call-done = f32[1,640,192]{1,2,0:T(8,128)} async-done(((f32[16,640,192]{1,2,0:T(8,128)}), f32[1,640,192]{1,2,0:T(8,128)}) %reduce-scatter.2.cloned.1.call-update) | async-done | bytes 491536 | tf_op jit(solution)/shard_map/reduce_scatter | solution.py:57
  284.1 1.3 copy.43
  285.3 19.8 %all_to_all.35 = f32[16,40,192]{2,1,0:T(8,128)S(1)} all-to-all(f32[16,40,192]{2,1,0:T(8,128)S(1)} %bitcast.58), channel_id=1, replica_groups=mesh['fsdp'=16,'expert'=16] {'expert'}, dimensions={0} | all-to-all | bytes 983040 | tf_op jit(solution)/shard_map/all_to_all | solution.py:59
  305.8 1.0 stack.2
  306.9 5.7 %all-to-all-start.3 = ((bf16[16,128,192]{1,2,0:T(8,128)(2,1)}), bf16[16,128,192]{1,2,0:T(8,128)(2,1)S(1)}, u32[]{:S(2)}, u32[]{:S(2)}) async-start(bf16[16,128,192]{1,2,0:T(8,128)(2,1)} %stack.2), calls=%async_computation.4 | async-start | bytes 1572864 | tf_op jit(solution)/shard_map/all_to_all | solution.py:73
  313.2 6.3 %fusion.4 = bf16[384,8,384]{0,2,1:T(8,128)(2,1)} fusion(bf16[16,640,384]{2,1,0:T(8,128)(2,1)} %all-gather.2.cloned.1.call-done, f32[640]{0:T(1024)S(1)} %mul.34, f32[640,384]{0,1:T(8,128)} %copy-done.3), kind=kOutput, calls=%fused_computation.5 | convolution fusion | flops 1512603648 | bytes 7277056 | tf_op jit(solution)/shard_map/sf,zsd->fzd/dot_general | solution.py:62
  319.5 4.3 %copy.49 = bf16[384,1,3072]{2,0,1:T(8,128)(2,1)} copy(bf16[384,1,3072]{0,2,1:T(8,128)(2,1)} %bitcast.61) | data formatting | bytes 4718592
  323.7 6.1 %convolution_convert_fusion = bf16[8,384,384]{2,1,0:T(8,128)(2,1)} fusion(bf16[16,640,384]{2,1,0:T(8,128)(2,1)} %all-gather.2.cloned.1.call-done, bf16[640,384]{0,1:T(8,128)(2,1)} %copy-done.2), kind=kOutput, calls=%fused_computation.6 | convolution fusion | flops 1511129088 | bytes 10715136 | tf_op jit(solution)/shard_map/zsd,sf->zdf/dot_general | solution.py:61
  329.8 2.5 all-to-all-done.3
  332.4 1.2 copy.48
  (30 shorter events, 4.2 us)
Async XLA Ops:
  7.2 114.7 %copy-start = (bf16[3072,1,384]{2,0,1:T(8,128)(2,1)S(1)}, bf16[3072,1,384]{2,0,1:T(8,128)(2,1)}, u32[]{:S(2)}) copy-start(bf16[3072,1,384]{2,0,1:T(8,128)(2,1)} %param.10) | copy-start | bytes 7077892
  7.2 24.2 %copy-start.5 = (bf16[128,4]{0,1:T(4,128)(2,1)S(1)}, bf16[128,4]{0,1:T(4,128)(2,1)}, u32[]{:S(2)}) copy-start(bf16[128,4]{0,1:T(4,128)(2,1)} %param.9) | copy-start | bytes 3076
  7.2 114.6 %all-gather.2.cloned.1.call-start = ((), (), s32[]{:S(2)}) async-start(), calls=%async_computation.6 | async-start | bytes 8355840 | tf_op jit(solution)/shard_map/all_gather | solution.py:43
  121.8 4.3 %copy-start.1 = (bf16[48,8,8,384]{3,2,1,0:T(8,128)(2,1)S(1)}, bf16[48,8,8,384]{3,2,1,0:T(8,128)(2,1)}, u32[]{:S(2)}) copy-start(bf16[48,8,8,384]{3,2,1,0:T(8,128)(2,1)} %copy.59) | copy-start | bytes 7077892
  121.8 5.1 %copy-start.6 = (bf16[16,640,384]{2,1,0:T(8,128)(2,1)S(1)}, bf16[16,640,384]{2,1,0:T(8,128)(2,1)}, u32[]{:S(2)}) copy-start(bf16[16,640,384]{2,1,0:T(8,128)(2,1)} %all-gather.2.cloned.1.call-done) | copy-start | bytes 23592964
  126.1 62.8 %copy-start.3 = (f32[640,384]{0,1:T(8,128)}, f32[640,384]{0,1:T(8,128)S(1)}, u32[]{:S(2)}) copy-start(f32[640,384]{0,1:T(8,128)S(1)} %convolution_bitcast_fusion.1) | copy-start | bytes 2949124
  127.0 42.8 %copy-start.4 = (s32[128,4]{0,1:T(4,128)S(1)}, s32[128,4]{0,1:T(4,128)}, u32[]{:S(2)}) copy-start(s32[128,4]{0,1:T(4,128)} %param.8) | copy-start | bytes 6148
  163.5 13.7 %all-to-all-start.4 = ((f32[16,1,40]{2,1,0:T(1,128)}), f32[16,1,40]{2,1,0:T(1,128)S(1)}, u32[]{:S(2)}, u32[]{:S(2)}) async-start(f32[16,1,40]{2,1,0:T(1,128)} %psum.7), calls=%async_computation.5 | async-start | bytes 16384 | tf_op jit(solution)/shard_map/all_to_all | solution.py:60
  169.7 114.4 %reduce-scatter.2.cloned.1.call-start = ((), (), s32[]{:S(2)}) async-start(), calls=%async_computation.7 | async-start | bytes 8355840 | tf_op jit(solution)/shard_map/reduce_scatter | solution.py:57
  190.5 0.8 copy-start.2
  306.9 25.5 %all-to-all-start.3 = ((bf16[16,128,192]{1,2,0:T(8,128)(2,1)}), bf16[16,128,192]{1,2,0:T(8,128)(2,1)S(1)}, u32[]{:S(2)}, u32[]{:S(2)}) async-start(bf16[16,128,192]{1,2,0:T(8,128)(2,1)} %stack.2), calls=%async_computation.4 | async-start | bytes 1572864 | tf_op jit(solution)/shard_map/all_to_all | solution.py:73
Sparse Core Ops, SparseCore 0:
  27.9 93.8 all-gather.1
  196.0 88.0 reduce-scatter.1
